TPU v7x, 256 devices: a whole 4x4x8 slice. The times are simulated.
256 devices in a mesh: dp: 16 (over z, core), expert: 16 (over y, x).
Axes of the slice: x: 4, y: 4, z: 8, core: 2. Of those that a mesh axis runs over, the one named last changes fastest.
Arguments:
- tokens: bfloat16 [32768, 2048], P(('dp', 'expert')), may hold values from -6 to 6
- expert_ids: int32 [32768, 2], P(('dp', 'expert')), may hold values from 0 to 7, all different within a row; in each aligned block of 128 rows (0 to 127, 128 to 255, ...) at most 40 rows name the same one
- gate_values: bfloat16 [32768, 2], P(('dp', 'expert')), may hold values from 0.19921875 to 0.796875
- w_gate: bfloat16 [16, 2048, 896], P('expert', 'dp'), may hold values from -0.125 to 0.125
- w_up: bfloat16 [16, 2048, 896], P('expert', 'dp'), may hold values from -0.125 to 0.125
- w_down: bfloat16 [16, 896, 2048], P('expert', 'dp'), may hold values from -0.0625 to 0.0625
- cotangent: bfloat16 [32768, 2048], P(('dp', 'expert')), may hold values from -6 to 6
- momentum: bfloat16 [16, 896, 2048], P('expert', 'dp'), may hold values from -4 to 4
- worker_error: bfloat16 [16, 16, 896, 2048], P('dp', 'expert'), may hold values from -2 to 2
- server_error: float32 [16, 896, 2048], P('expert', 'dp'), may hold values from -2 to 2
Outputs:
- outputs: bfloat16 [32768, 2048], P(('dp', 'expert'))
- new_momentum: bfloat16 [16, 896, 2048], P('expert', 'dp')
- new_worker_error: bfloat16 [16, 16, 896, 2048], P('dp', 'expert')
- new_server_error: float32 [16, 896, 2048], P('expert', 'dp')
Inputs may be any that keep to these rules, and one draw needn't show every extreme that they name: `expert_ids`: A token names 2 different experts. Among the 128 tokens of one device at most 40 name the same expert, and some device reaches 40.
All inputs are finite; a program needn't handle non-finite values. Where the computation divides by a largest or mean magnitude, that divisor is 1e-20 or more.
Results may differ from a plain program's by a relative error of at most 0.009.
Values may be sent and summed in bfloat16 or wider, within the bound.
No kernel may reach another device: no remote copies, remote signals or barrier semaphores. Data moves between devices by JAX's collectives and lax.ppermute only.
A program may use at most 128 MiB of HBM per device.

v0:
```python
import jax
import jax.numpy as jnp
import numpy as np
from jax import lax
from jax.sharding import PartitionSpec as P

E = 8
EW = 2
TOP = 2
CAP = 40


def squash(values):
    scale = jnp.mean(jnp.abs(values), axis=-1, keepdims=True) + 1e-06
    return (scale * jnp.tanh(values / scale)).astype(jnp.bfloat16)


def per_device(
    tokens,
    expert_ids,
    gate_values,
    w_gate,
    w_up,
    w_down,
    cotangent,
    momentum,
    worker_error,
    server_error,
):
    n_expert = lax.axis_size("expert")
    n_replica = lax.axis_size("dp")
    tok_count = tokens.shape[0]
    width = tokens.shape[1]
    hidden_units = w_gate.shape[2]
    slots = EW * CAP
    share = n_expert // EW
    flat = expert_ids.reshape(-1)
    onehot = (flat[:, None] == jnp.arange(E, dtype=jnp.int32)[None, :]).astype(jnp.int32)
    ranks = jnp.sum((jnp.cumsum(onehot, axis=0) - onehot) * onehot, axis=1)
    position = jnp.where(flat < EW, flat * CAP + ranks, -1)
    select = (position[None, :] == jnp.arange(slots, dtype=jnp.int32)[:, None]).reshape(
        slots, tok_count, TOP
    )
    dispatch = jnp.any(select, axis=2).astype(jnp.bfloat16)
    combine_w = jnp.sum(jnp.where(select, gate_values.astype(jnp.float32)[None], 0.0), axis=2)
    slot_gates = jnp.sum(combine_w, axis=1).astype(jnp.bfloat16).reshape(EW, CAP)
    peer_owner = np.arange(n_expert) // share
    mix = jnp.asarray((peer_owner[:, None] == np.arange(EW)[None, :]).astype(np.float32)).astype(
        jnp.bfloat16
    )

    def spread(buffer):
        return jnp.take(buffer, jnp.asarray(peer_owner, dtype=jnp.int32), axis=0)

    def slot_rows(source):
        return (
            jnp.dot(dispatch, source, preferred_element_type=jnp.float32)
            .astype(jnp.bfloat16)
            .reshape(EW, CAP, width)
        )

    send_rows = spread(slot_rows(tokens))
    send_gates = spread(slot_gates)
    got_rows, got_gates = (
        lax.all_to_all(send_rows, "expert", split_axis=0, concat_axis=0, tiled=True),
        lax.all_to_all(send_gates, "expert", split_axis=0, concat_axis=0, tiled=True),
    )
    rows = got_rows.reshape(n_expert * CAP, width)
    pieces = (
        lax.all_gather(w_gate, "dp", axis=1, tiled=True),
        lax.all_gather(w_up, "dp", axis=1, tiled=True),
    )
    gate_h = jnp.dot(rows, pieces[0][0], preferred_element_type=jnp.float32)
    up_h = jnp.dot(rows, pieces[1][0], preferred_element_type=jnp.float32)
    hidden = (jax.nn.silu(gate_h) * up_h).astype(jnp.bfloat16)
    down_full, mom_full = (
        lax.all_gather(w_down, "dp", axis=1, tiled=True),
        lax.all_gather(momentum, "dp", axis=1, tiled=True),
    )
    partial_value = jnp.dot(hidden, down_full[0], preferred_element_type=jnp.float32).astype(
        jnp.bfloat16
    )
    returned = lax.all_to_all(
        partial_value.reshape(n_expert, CAP, width),
        "expert",
        split_axis=0,
        concat_axis=0,
        tiled=True,
    )
    expert_sum = jnp.einsum("kcd,ke->ecd", returned, mix, preferred_element_type=jnp.float32)
    outputs = jnp.einsum(
        "pt,pd->td",
        combine_w,
        expert_sum.reshape(slots, width),
        precision=lax.Precision.HIGHEST,
        preferred_element_type=jnp.float32,
    ).astype(jnp.bfloat16)
    got_cot = lax.all_to_all(
        spread(slot_rows(cotangent)), "expert", split_axis=0, concat_axis=0, tiled=True
    )
    dy_rows = got_cot.reshape(n_expert * CAP, width)
    gate_rows = got_gates.reshape(n_expert * CAP).astype(jnp.float32)
    weighted = (hidden.astype(jnp.float32) * gate_rows[:, None]).astype(jnp.bfloat16)
    grad = jnp.einsum("rh,rd->hd", weighted, dy_rows, preferred_element_type=jnp.float32)
    corrected = (
        0.9 * mom_full[0].astype(jnp.float32) + 0.1 * grad + worker_error[0, 0].astype(jnp.float32)
    )
    sent = squash(corrected)
    new_worker = (corrected - sent.astype(jnp.float32)).astype(jnp.bfloat16)[None, None]
    pieces = sent.reshape(n_replica, hidden_units // n_replica, width)
    received = lax.all_to_all(pieces, "dp", split_axis=0, concat_axis=0, tiled=True)
    average = jnp.sum(received.astype(jnp.float32), axis=0) / n_replica
    server_in = average + server_error[0]
    served = squash(server_in)
    new_server = (server_in - served.astype(jnp.float32))[None]
    return (outputs, served[None], new_worker, new_server)


def solution(mesh):
    return jax.shard_map(
        per_device,
        mesh=mesh,
        in_specs=(
            P(("dp", "expert"), None),
            P(("dp", "expert"), None),
            P(("dp", "expert"), None),
            P("expert", "dp", None),
            P("expert", "dp", None),
            P("expert", "dp", None),
            P(("dp", "expert"), None),
            P("expert", "dp", None),
            P("dp", "expert", None, None),
            P("expert", "dp", None),
        ),
        out_specs=(
            P(("dp", "expert"), None),
            P("expert", "dp", None),
            P("dp", "expert", None, None),
            P("expert", "dp", None),
        ),
        check_vma=False,
    )
```

profile of v0, /device:TPU:1, one launch (start us, length us, event | category | flops | bytes accessed | tf_op | source)
XLA Modules:
  0.0 293.4 jit_solution(15084399947835725456)
XLA Ops:
  7.2 0.7 all-gather.5.cloned.1.call-update
  8.0 0.7 all-gather.7.cloned.1.call-update
  8.7 0.7 all-gather.9.cloned.1.call-update
  9.4 0.5 all-gather.11.cloned.1.call-update
  10.0 0.8 copy.50
  10.8 0.1 eq.43
  10.9 0.1 eq.39
  11.0 0.7 convert_element_type.85
  11.7 0.6 reduce-window.6
  12.3 0.2 slice_reduce_fusion
  12.5 0.1 fusion.19
  12.6 0.1 reduce_sum.57
  12.8 0.7 compare_select_fusion
  13.5 0.1 select_reduce_fusion
  13.7 0.1 convert_element_type.94
  13.7 0.7 pad_clamp_fusion
  14.4 0.6 gather_fusion
  15.0 0.6 copy.55
  15.6 7.6 %all-to-all-start.2 = ((bf16[16,1,40]{2,1,0:T(2,128)(2,1)}), bf16[16,1,40]{2,1,0:T(2,128)(2,1)S(1)}, u32[]{:S(2)}, u32[]{:S(2)}) async-start(bf16[16,1,40]{2,1,0:T(2,128)(2,1)} %copy.55), calls=%async_computation.2 | async-start | bytes 16384 | tf_op jit(solution)/shard_map/all_to_all | solution.py:66
  23.2 0.2 convolution_convert_fusion.2
  23.5 2.2 gather_fusion.1
  25.7 3.8 %all-to-all-done.2 = bf16[16,1,40]{2,1,0:T(2,128)(2,1)S(1)} async-done(((bf16[16,1,40]{2,1,0:T(2,128)(2,1)}), bf16[16,1,40]{2,1,0:T(2,128)(2,1)S(1)}, u32[]{:S(2)}, u32[]{:S(2)}) %all-to-all-start.2) | async-done | bytes 1312 | tf_op jit(solution)/shard_map/all_to_all | solution.py:66
  29.5 3.8 %all-to-all-start = ((bf16[16,40,2048]{2,1,0:T(8,128)(2,1)}), bf16[16,40,2048]{2,1,0:T(8,128)(2,1)S(1)}, u32[]{:S(2)}, u32[]{:S(2)}) async-start(bf16[16,40,2048]{2,1,0:T(8,128)(2,1)} %gather_fusion.1), calls=%async_computation | async-start | bytes 5242880 | tf_op jit(solution)/shard_map/all_to_all | solution.py:65
  33.3 1.3 convolution_convert_fusion.1
  34.6 2.2 gather_fusion.2
  36.8 31.5 %all-to-all-done = bf16[16,40,2048]{2,1,0:T(8,128)(2,1)S(1)} async-done(((bf16[16,40,2048]{2,1,0:T(8,128)(2,1)}), bf16[16,40,2048]{2,1,0:T(8,128)(2,1)S(1)}, u32[]{:S(2)}, u32[]{:S(2)}) %all-to-all-start) | async-done | bytes 2621472 | tf_op jit(solution)/shard_map/all_to_all | solution.py:65
  68.3 1.5 copy-done.2
  69.8 5.5 %all-to-all-start.3 = ((bf16[16,40,2048]{2,1,0:T(8,128)(2,1)}), bf16[16,40,2048]{2,1,0:T(8,128)(2,1)S(1)}, u32[]{:S(2)}, u32[]{:S(2)}) async-start(bf16[16,40,2048]{2,1,0:T(8,128)(2,1)} %gather_fusion.2), calls=%async_computation.3 | async-start | bytes 5242880 | tf_op jit(solution)/shard_map/all_to_all | solution.py:98
  75.3 7.2 %fusion.5 = f32[640,896]{1,0:T(8,128)} fusion(bf16[640,2048]{1,0:T(8,128)(2,1)} %bitcast.68, bf16[1,2048,896]{2,1,0:T(8,128)(2,1)} %all-gather.5.cloned.1.call-done), kind=kOutput, calls=%fused_computation.14 | convolution fusion | flops 2348810240 | bytes 8585216 | tf_op jit(solution)/shard_map/dot_general | solution.py:73
  82.5 14.8 %all-gather.7.cloned.1.call-done = bf16[1,2048,896]{2,1,0:T(8,128)(2,1)} async-done(((bf16[1,128,896]{2,1,0:T(8,128)(2,1)}), bf16[1,2048,896]{2,1,0:T(8,128)(2,1)}) %all-gather.7.cloned.1.call-update) | async-done | bytes 3670032 | tf_op jit(solution)/shard_map/all_gather | solution.py:71
  97.3 7.5 %multiply_convert_fusion.2 = bf16[640,896]{1,0:T(8,128)(2,1)} fusion(f32[640,896]{1,0:T(8,128)} %fusion.5, bf16[640,2048]{1,0:T(8,128)(2,1)} %bitcast.69, bf16[1,2048,896]{2,1,0:T(8,128)(2,1)} %all-gather.7.cloned.1.call-done), kind=kOutput, calls=%fused_computation.23 | convolution fusion | flops 2352250880 | bytes 9732096 | tf_op jit(solution)/shard_map/dot_general | solution.py:74
  104.8 35.1 %all-gather.9.cloned.1.call-done = bf16[1,896,2048]{2,1,0:T(8,128)(2,1)} async-done(((bf16[1,56,2048]{2,1,0:T(8,128)(2,1)}), bf16[1,896,2048]{2,1,0:T(8,128)(2,1)}) %all-gather.9.cloned.1.call-update) | async-done | bytes 3670032 | tf_op jit(solution)/shard_map/all_gather | solution.py:77
  139.8 6.8 %fusion.7 = bf16[640,2048]{1,0:T(8,128)(2,1)} fusion(bf16[640,896]{1,0:T(8,128)(2,1)} %multiply_convert_fusion.2, bf16[1,896,2048]{2,1,0:T(8,128)(2,1)} %all-gather.9.cloned.1.call-done), kind=kOutput, calls=%fused_computation.16 | convolution fusion | flops 2350120960 | bytes 7438336 | tf_op jit(solution)/shard_map/dot_general | solution.py:80
  146.6 1.5 copy-done.1
  148.1 6.5 %all-to-all-start.1 = ((bf16[16,40,2048]{2,1,0:T(8,128)(2,1)}), bf16[16,40,2048]{2,1,0:T(8,128)(2,1)S(1)}, u32[]{:S(2)}, u32[]{:S(2)}) async-start(bf16[16,40,2048]{2,1,0:T(8,128)(2,1)} %bitcast.67), calls=%async_computation.1 | async-start | bytes 5242880 | tf_op jit(solution)/shard_map/all_to_all | solution.py:83
  154.7 0.1 reshape.180
  154.8 26.9 %all-gather.11.cloned.1.call-done = bf16[1,896,2048]{2,1,0:T(8,128)(2,1)} async-done(((bf16[1,56,2048]{2,1,0:T(8,128)(2,1)}), bf16[1,896,2048]{2,1,0:T(8,128)(2,1)}) %all-gather.11.cloned.1.call-update) | async-done | bytes 3670032 | tf_op jit(solution)/shard_map/all_gather | solution.py:78
  181.7 8.9 %abs_reduce_fusion = (f32[896]{0:T(1024)S(1)}, f32[896,2048]{1,0:T(8,128)S(1)}) fusion(bf16[1,1,896,2048]{3,2,1,0:T(8,128)(2,1)} %param.24, bf16[640,2048]{1,0:T(8,128)(2,1)} %bitcast.66, bf16[640,896]{1,0:T(8,128)(2,1)} %multiply_convert_fusion.2, f32[640]{0:T(1024)S(1)} %reshape.180, bf16[1,896,2048]{2,1,0:T(8,128)(2,1)} %all-gather.11.cloned.1.call-done), kind=kOutput, calls=%fused_computation.8 | convolution fusion | flops 2365209600 | bytes 18454528 | tf_op jit(solution)/shard_map/rh,rd->hd/dot_general | solution.py:104
  190.6 3.9 %fusion = (bf16[1,1,896,2048]{3,2,1,0:T(8,128)(2,1)}, bf16[896,2048]{1,0:T(8,128)(2,1)}) fusion(f32[896,2048]{1,0:T(8,128)S(1)} %get-tuple-element.12, f32[896]{0:T(1024)S(1)} %multiply_add_fusion), kind=kLoop, calls=%fused_computation.9 | loop fusion | flops 11010048 | bytes 14683648 | tf_op jit(solution)/shard_map/broadcast_in_dim | solution.py:109
  194.5 0.3 all-to-all-done.1
  194.7 5.8 %all-to-all-start.4 = ((bf16[16,56,2048]{2,1,0:T(8,128)(2,1)}), bf16[16,56,2048]{2,1,0:T(8,128)(2,1)}, u32[]{:S(2)}, u32[]{:S(2)}) async-start(bf16[16,56,2048]{2,1,0:T(8,128)(2,1)} %bitcast.65), calls=%async_computation.4 | async-start | bytes 7340032 | tf_op jit(solution)/shard_map/all_to_all | solution.py:111
  200.6 3.0 %fusion.10 = f32[2,40,2048]{2,0,1:T(2,128)S(1)} fusion(bf16[16,2,1]{0,1,2:T(2,128)(2,1)S(1)} %copy-done.4, bf16[16,40,2048]{2,1,0:T(8,128)(2,1)S(1)} %all-to-all-done.1), kind=kOutput, calls=%fused_computation.17 | convolution fusion | flops 5242880 | bytes 3276864 | tf_op jit(solution)/shard_map/kcd,ke->ecd/dot_general | solution.py:90
  203.5 0.4 copy.54
  203.9 1.8 convolution_convert_fusion
  205.8 77.2 %all-to-all-done.4 = bf16[16,56,2048]{2,1,0:T(8,128)(2,1)} async-done(((bf16[16,56,2048]{2,1,0:T(8,128)(2,1)}), bf16[16,56,2048]{2,1,0:T(8,128)(2,1)}, u32[]{:S(2)}, u32[]{:S(2)}) %all-to-all-start.4) | async-done | bytes 3670048 | tf_op jit(solution)/shard_map/all_to_all | solution.py:111
  282.9 2.8 convert_reduce_fusion
  285.7 0.2 fusion.16
  285.9 1.0 convert_subtract_fusion
  (22 shorter events, 0.4 us)
Async XLA Ops:
  7.2 16.0 %copy-start = (bf16[128,2048]{1,0:T(8,128)(2,1)S(1)}, bf16[128,2048]{1,0:T(8,128)(2,1)}, u32[]{:S(2)}) copy-start(bf16[128,2048]{1,0:T(8,128)(2,1)} %param.16) | copy-start | bytes 1572868
  7.2 68.2 %all-gather.5.cloned.1.call-start = ((), (), s32[]{:S(2)}) async-start(), calls=%async_computation.5 | async-start | bytes 3899392 | tf_op jit(solution)/shard_map/all_gather | solution.py:70
  7.9 89.4 %all-gather.7.cloned.1.call-start = ((), (), s32[]{:S(2)}) async-start(), calls=%async_computation.6 | async-start | bytes 3899392 | tf_op jit(solution)/shard_map/all_gather | solution.py:71
  8.7 131.2 %all-gather.9.cloned.1.call-start = ((), (), s32[]{:S(2)}) async-start(), calls=%async_computation.7 | async-start | bytes 3899392 | tf_op jit(solution)/shard_map/all_gather | solution.py:77
  9.4 172.3 %all-gather.11.cloned.1.call-start = ((), (), s32[]{:S(2)}) async-start(), calls=%async_computation.8 | async-start | bytes 3899392 | tf_op jit(solution)/shard_map/all_gather | solution.py:78
  15.6 13.9 %all-to-all-start.2 = ((bf16[16,1,40]{2,1,0:T(2,128)(2,1)}), bf16[16,1,40]{2,1,0:T(2,128)(2,1)S(1)}, u32[]{:S(2)}, u32[]{:S(2)}) async-start(bf16[16,1,40]{2,1,0:T(2,128)(2,1)} %copy.55), calls=%async_computation.2 | async-start | bytes 16384 | tf_op jit(solution)/shard_map/all_to_all | solution.py:66
  29.5 38.8 %all-to-all-start = ((bf16[16,40,2048]{2,1,0:T(8,128)(2,1)}), bf16[16,40,2048]{2,1,0:T(8,128)(2,1)S(1)}, u32[]{:S(2)}, u32[]{:S(2)}) async-start(bf16[16,40,2048]{2,1,0:T(8,128)(2,1)} %gather_fusion.1), calls=%async_computation | async-start | bytes 5242880 | tf_op jit(solution)/shard_map/all_to_all | solution.py:65
  68.3 1.5 copy-start.2
  69.8 76.9 %all-to-all-start.3 = ((bf16[16,40,2048]{2,1,0:T(8,128)(2,1)}), bf16[16,40,2048]{2,1,0:T(8,128)(2,1)S(1)}, u32[]{:S(2)}, u32[]{:S(2)}) async-start(bf16[16,40,2048]{2,1,0:T(8,128)(2,1)} %gather_fusion.2), calls=%async_computation.3 | async-start | bytes 5242880 | tf_op jit(solution)/shard_map/all_to_all | solution.py:98
  146.6 1.5 copy-start.1
  148.1 46.6 %all-to-all-start.1 = ((bf16[16,40,2048]{2,1,0:T(8,128)(2,1)}), bf16[16,40,2048]{2,1,0:T(8,128)(2,1)S(1)}, u32[]{:S(2)}, u32[]{:S(2)}) async-start(bf16[16,40,2048]{2,1,0:T(8,128)(2,1)} %bitcast.67), calls=%async_computation.1 | async-start | bytes 5242880 | tf_op jit(solution)/shard_map/all_to_all | solution.py:83
  194.7 5.8 %copy-start.4 = (bf16[16,2,1]{0,1,2:T(2,128)(2,1)S(1)}, bf16[16,2,1]{0,1,2:T(2,128)(2,1)}, u32[]{:S(2)}) copy-start(bf16[16,2,1]{0,1,2:T(2,128)(2,1)} %constant.104) | copy-start | bytes 196
  194.7 88.2 %all-to-all-start.4 = ((bf16[16,56,2048]{2,1,0:T(8,128)(2,1)}), bf16[16,56,2048]{2,1,0:T(8,128)(2,1)}, u32[]{:S(2)}, u32[]{:S(2)}) async-start(bf16[16,56,2048]{2,1,0:T(8,128)(2,1)} %bitcast.65), calls=%async_computation.4 | async-start | bytes 7340032 | tf_op jit(solution)/shard_map/all_to_all | solution.py:111
  203.9 81.8 %copy-start.3 = (f32[1,56,2048]{2,1,0:T(8,128)S(1)}, f32[1,56,2048]{2,1,0:T(8,128)}, u32[]{:S(2)}) copy-start(f32[1,56,2048]{2,1,0:T(8,128)} %param.25) | copy-start | bytes 1376260
Sparse Core Ops, SparseCore 0:
  9.8 45.3 all-gather.4
  57.1 40.1 all-gather.6
  99.1 40.6 all-gather.8
  141.5 40.1 all-gather.10
where the time goes:
time: 294 us; the launch traced here: 293 us
  waiting for transfers between devices  192 us (65%)
  matrix products  36.6 us (12%)
  starting transfers between devices  29.4 us (10%)
  between operations  13.9 us (5%)
  other arithmetic  10.7 us (4%)
  local copies, waits for them, and re-layouts  10.6 us (4%)
    all_to_all x1, waiting for transfers between devices, per_device(): lax.all_to_all(pieces, 'dp', split_axis=0, concat_axis=0, tiled=True)  77.2 us
    all_gather x1, waiting for transfers between devices, per_device(): lax.all_gather(w_down, 'dp', axis=1, tiled=True)  35.1 us
    all_to_all x1, waiting for transfers between devices, per_device(): lax.all_to_all(send_rows, 'expert', split_axis=0, concat_axis=0, tiled=True)  31.5 us
    all_gather x1, waiting for transfers between devices, per_device(): lax.all_gather(momentum, 'dp', axis=1, tiled=True)  26.9 us
    all_gather x1, waiting for transfers between devices, per_device(): lax.all_gather(w_up, 'dp', axis=1, tiled=True)  14.8 us
    dot_general x1, matrix products, per_device(): jnp.einsum('rh,rd->hd', weighted, dy_rows, preferred_element_type=jnp.flo...  8.87 us
    all_to_all x1, starting transfers between devices, per_device(): lax.all_to_all(send_gates, 'expert', split_axis=0, concat_axis=0, tiled=T...  7.58 us
    dot_general x1, matrix products, per_device(): up_h = jnp.dot(rows, pieces[1][0], preferred_element_type=jnp.float32)  7.46 us
  transfers between devices with their start and end apart: 9, of which 7 were waited for; matrix products, arithmetic and copies ran while one was open for 17% of the time, Pallas kernels for 0%

commit v1 on v0

--- a/solution.py
+++ b/solution.py
@@ -2,6 +2,7 @@
 import jax.numpy as jnp
 import numpy as np
 from jax import lax
+from jax.sharding import Mesh
 from jax.sharding import PartitionSpec as P
 
 E = 8
@@ -13,6 +14,21 @@
 def squash(values):
     scale = jnp.mean(jnp.abs(values), axis=-1, keepdims=True) + 1e-06
     return (scale * jnp.tanh(values / scale)).astype(jnp.bfloat16)
+
+
+def swap_cores(value):
+    return lax.ppermute(value, "core", [(0, 1), (1, 0)])
+
+
+def gather_halves(piece):
+    own = lax.all_gather(piece, "z", axis=0, tiled=False)
+    return own, swap_cores(own)
+
+
+def in_order(own, other):
+    first = lax.axis_index("core") == 0
+    pair = jnp.stack([jnp.where(first, own, other), jnp.where(first, other, own)], axis=1)
+    return pair.reshape(-1, pair.shape[-1])
 
 
 def per_device(
@@ -28,7 +44,9 @@
     server_error,
 ):
     n_expert = lax.axis_size("expert")
-    n_replica = lax.axis_size("dp")
+    n_z = lax.axis_size("z")
+    n_replica = n_z * lax.axis_size("core")
+    core = lax.axis_index("core")
     tok_count = tokens.shape[0]
     width = tokens.shape[1]
     hidden_units = w_gate.shape[2]
@@ -59,25 +77,36 @@
             .reshape(EW, CAP, width)
         )
 
-    send_rows = spread(slot_rows(tokens))
+    by_core = tokens.reshape(tok_count, n_z, 2, -1)
+    even = by_core[:, :, 0].reshape(tok_count, width // 2)
+    odd = by_core[:, :, 1].reshape(tok_count, width // 2)
+    own_first = jnp.concatenate(
+        [jnp.where(core == 0, even, odd), jnp.where(core == 0, odd, even)], axis=1
+    )
+    send_rows = spread(slot_rows(own_first))
     send_gates = spread(slot_gates)
     got_rows, got_gates = (
         lax.all_to_all(send_rows, "expert", split_axis=0, concat_axis=0, tiled=True),
         lax.all_to_all(send_gates, "expert", split_axis=0, concat_axis=0, tiled=True),
     )
     rows = got_rows.reshape(n_expert * CAP, width)
-    pieces = (
-        lax.all_gather(w_gate, "dp", axis=1, tiled=True),
-        lax.all_gather(w_up, "dp", axis=1, tiled=True),
-    )
-    gate_h = jnp.dot(rows, pieces[0][0], preferred_element_type=jnp.float32)
-    up_h = jnp.dot(rows, pieces[1][0], preferred_element_type=jnp.float32)
+    gate_own, gate_other = gather_halves(w_gate[0])
+    up_own, up_other = gather_halves(w_up[0])
+
+    def project(own, other):
+        half = width // 2
+        return jnp.dot(
+            rows[:, :half], own.reshape(half, hidden_units), preferred_element_type=jnp.float32
+        ) + jnp.dot(
+            rows[:, half:], other.reshape(half, hidden_units), preferred_element_type=jnp.float32
+        )
+
+    gate_h = project(gate_own, gate_other)
+    up_h = project(up_own, up_other)
     hidden = (jax.nn.silu(gate_h) * up_h).astype(jnp.bfloat16)
-    down_full, mom_full = (
-        lax.all_gather(w_down, "dp", axis=1, tiled=True),
-        lax.all_gather(momentum, "dp", axis=1, tiled=True),
-    )
-    partial_value = jnp.dot(hidden, down_full[0], preferred_element_type=jnp.float32).astype(
+    down_full = in_order(*gather_halves(w_down[0]))
+    mom_full = in_order(*gather_halves(momentum[0]))
+    partial_value = jnp.dot(hidden, down_full, preferred_element_type=jnp.float32).astype(
         jnp.bfloat16
     )
     returned = lax.all_to_all(
@@ -103,13 +132,18 @@
     weighted = (hidden.astype(jnp.float32) * gate_rows[:, None]).astype(jnp.bfloat16)
     grad = jnp.einsum("rh,rd->hd", weighted, dy_rows, preferred_element_type=jnp.float32)
     corrected = (
-        0.9 * mom_full[0].astype(jnp.float32) + 0.1 * grad + worker_error[0, 0].astype(jnp.float32)
+        0.9 * mom_full.astype(jnp.float32) + 0.1 * grad + worker_error[0, 0].astype(jnp.float32)
     )
     sent = squash(corrected)
     new_worker = (corrected - sent.astype(jnp.float32)).astype(jnp.bfloat16)[None, None]
-    pieces = sent.reshape(n_replica, hidden_units // n_replica, width)
-    received = lax.all_to_all(pieces, "dp", split_axis=0, concat_axis=0, tiled=True)
-    average = jnp.sum(received.astype(jnp.float32), axis=0) / n_replica
+    pieces = sent.reshape(n_z, 2, hidden_units // n_replica, width)
+    kept = jnp.where(core == 0, pieces[:, 0], pieces[:, 1])
+    passed = jnp.where(core == 0, pieces[:, 1], pieces[:, 0])
+    pair_sum = (kept.astype(jnp.float32) + swap_cores(passed).astype(jnp.float32)).astype(
+        jnp.bfloat16
+    )
+    total = lax.psum_scatter(pair_sum, "z", scatter_dimension=0, tiled=False)
+    average = total.astype(jnp.float32) / n_replica
     server_in = average + server_error[0]
     served = squash(server_in)
     new_server = (server_in - served.astype(jnp.float32))[None]
@@ -117,26 +151,28 @@
 
 
 def solution(mesh):
+    shape = (mesh.shape["dp"] // 2, 2, mesh.shape["expert"])
+    split = Mesh(mesh.devices.reshape(shape), ("z", "core", "expert"))
     return jax.shard_map(
         per_device,
-        mesh=mesh,
+        mesh=split,
         in_specs=(
-            P(("dp", "expert"), None),
-            P(("dp", "expert"), None),
-            P(("dp", "expert"), None),
-            P("expert", "dp", None),
-            P("expert", "dp", None),
-            P("expert", "dp", None),
-            P(("dp", "expert"), None),
-            P("expert", "dp", None),
-            P("dp", "expert", None, None),
-            P("expert", "dp", None),
+            P(("z", "core", "expert"), None),
+            P(("z", "core", "expert"), None),
+            P(("z", "core", "expert"), None),
+            P("expert", ("z", "core"), None),
+            P("expert", ("z", "core"), None),
+            P("expert", ("z", "core"), None),
+            P(("z", "core", "expert"), None),
+            P("expert", ("z", "core"), None),
+            P(("z", "core"), "expert", None, None),
+            P("expert", ("z", "core"), None),
         ),
         out_specs=(
-            P(("dp", "expert"), None),
-            P("expert", "dp", None),
-            P("dp", "expert", None, None),
-            P("expert", "dp", None),
+            P(("z", "core", "expert"), None),
+            P("expert", ("z", "core"), None),
+            P(("z", "core"), "expert", None, None),
+            P("expert", ("z", "core"), None),
         ),
         check_vma=False,
     )

time: 294 us -> 273 us (0.929)
  waiting for transfers between devices: 192 us -> 116 us
  blocking collectives: 0 us -> 40.1 us
  other arithmetic: 10.7 us -> 19.2 us
  starting transfers between devices: 29.4 us -> 35.7 us
  matrix products: 36.6 us -> 31.6 us
  local copies, waits for them, and re-layouts: 10.6 us -> 15.6 us
    all_to_all x2 -> x0, waiting for transfers between devices: 77.5 us -> none  [the longest x1 77.2 us: per_device(): lax.all_to_all(pieces, 'dp', split_axis=0, concat_axis=0, tiled=True)]
    all_to_all x0 -> x1, blocking collectives: none -> 40.1 us  [per_device(): lax.all_to_all(partial_value.reshape(n_expert, CAP, width), 'expert', spl...]
    all_gather x4, waiting for transfers between devices: 76.8 us -> 112 us  [gather_halves(): own = lax.all_gather(piece, 'z', axis=0, tiled=False)]
    all_to_all x1, waiting for transfers between devices: 31.5 us -> 0.01 us  [per_device(): lax.all_to_all(send_rows, 'expert', split_axis=0, concat_axis=0, tiled=True)]
    ppermute x0 -> x5, starting transfers between devices: none -> 16.5 us  [swap_cores(): return lax.ppermute(value, 'core', [(0, 1), (1, 0)])]
    all_to_all x2 -> x0, starting transfers between devices: 12.4 us -> none  [the longest x1 6.53 us: per_device(): lax.all_to_all(partial_value.reshape(n_expert, CAP, width), 'expert', spl...]
    another operation x2 -> x5, other arithmetic: 0.61 us -> 7.3 us  [the longest x3 6.68 us: in_order(): jnp.stack([jnp.where(first, own, other), jnp.where(first, other, own)], a...]
    mul x0 -> x1, local copies, waits for them, and re-layouts: none -> 3.88 us  [per_device(): 0.9 * mom_full.astype(jnp.float32) + 0.1 * grad]
  transfers between devices with their start and end apart: 9 -> 13, of which waited for: 7 -> 5; matrix products, arithmetic and copies ran while one was open for 17% -> 21% of each run, Pallas kernels for 0% -> 0%
where the time goes in v1:
time: 273 us; the launch traced here: 272 us
  waiting for transfers between devices  116 us (42%)
  blocking collectives  40.1 us (15%)
  starting transfers between devices  35.7 us (13%)
  matrix products  31.6 us (12%)
  other arithmetic  19.2 us (7%)
  local copies, waits for them, and re-layouts  15.6 us (6%)
  between operations  14 us (5%)
    all_gather x4, waiting for transfers between devices, gather_halves(): own = lax.all_gather(piece, 'z', axis=0, tiled=False)  112 us
    all_to_all x1, blocking collectives, per_device(): lax.all_to_all(partial_value.reshape(n_expert, CAP, width), 'expert', spl...  40.1 us
    ppermute x5, starting transfers between devices, swap_cores(): return lax.ppermute(value, 'core', [(0, 1), (1, 0)])  16.5 us
    dot_general x2, matrix products, project(): jnp.dot(rows[:, :half], own.reshape(half, hidden_units), preferred_elemen...  8.31 us
    all_to_all x1, starting transfers between devices, per_device(): lax.all_to_all(send_gates, 'expert', split_axis=0, concat_axis=0, tiled=T...  7.58 us
    dot_general x1, matrix products, per_device(): jnp.einsum('rh,rd->hd', weighted, dy_rows, preferred_element_type=jnp.flo...  7.55 us
    dot_general x2, matrix products, project(): jnp.dot(rows[:, half:], other.reshape(half, hidden_units), preferred_elem...  7.37 us
    another operation x3, other arithmetic, in_order(): jnp.stack([jnp.where(first, own, other), jnp.where(first, other, own)], a...  6.68 us
  transfers between devices with their start and end apart: 13, of which 5 were waited for; matrix products, arithmetic and copies ran while one was open for 21% of the time, Pallas kernels for 0%

profile of v1, /device:TPU:1, one launch (start us, length us, event | category | flops | bytes accessed | tf_op | source)
XLA Modules:
  0.0 272.2 jit_solution(6642737530163769953)
XLA Ops:
  7.2 0.7 all-gather.11.cloned.1.call-update
  8.0 0.7 all-gather.5.cloned.1.call-update
  8.7 0.7 all-gather.7.cloned.1.call-update
  9.4 0.8 copy.81
  10.5 0.6 reduce-window.6
  11.6 0.7 convert_element_type.100
  12.3 0.7 compare_select_fusion
  13.2 0.7 pad_clamp_fusion
  13.9 0.6 gather_fusion
  14.4 0.6 copy.89
  15.0 7.6 %all-to-all-start.2 = ((bf16[16,1,40]{2,1,0:T(2,128)(2,1)}), bf16[16,1,40]{2,1,0:T(2,128)(2,1)S(1)}, u32[]{:S(2)}, u32[]{:S(2)}) async-start(bf16[16,1,40]{2,1,0:T(2,128)(2,1)} %copy.89), calls=%async_computation.2 | async-start | bytes 16384 | tf_op jit(solution)/shard_map/all_to_all | solution.py:90
  22.7 0.5 all-gather.9.cloned.1.call-update
  23.2 1.3 copy.84
  24.6 0.3 convolution_convert_fusion.3
  24.9 2.2 gather_fusion.1
  27.1 1.8 all-to-all-done.2
  29.0 4.8 %all-to-all-start = ((bf16[16,40,2048]{2,1,0:T(8,128)(2,1)}), bf16[16,40,2048]{2,1,0:T(8,128)(2,1)S(1)}, u32[]{:S(2)}, u32[]{:S(2)}) async-start(bf16[16,40,2048]{2,1,0:T(8,128)(2,1)} %gather_fusion.1), calls=%async_computation | async-start | bytes 5242880 | tf_op jit(solution)/shard_map/all_to_all | solution.py:89
  33.8 16.8 %all-gather.11.cloned.1.call-done = bf16[8,56,2048]{2,1,0:T(8,128)(2,1)} async-done(((bf16[1,56,2048]{2,1,0:T(8,128)(2,1)}), bf16[8,56,2048]{2,1,0:T(8,128)(2,1)}) %all-gather.11.cloned.1.call-update) | async-done | bytes 1835024 | tf_op jit(solution)/shard_map/all_gather | solution.py:24
  50.6 3.9 %collective-permute-start.3 = (bf16[8,56,2048]{2,1,0:T(8,128)(2,1)}, bf16[8,56,2048]{2,1,0:T(8,128)(2,1)}, u32[]{:S(2)}, u32[]{:S(2)}) collective-permute-start(bf16[8,56,2048]{2,1,0:T(8,128)(2,1)} %all-gather.11.cloned.1.call-done), channel_id=1, source_target_pairs={{0,16},{16,0},{1,17},{17,1},{2,18},{18,2},{3,19},{19,3},{4,20},{20... | collective-permute-start | bytes 5505032 | tf_op jit(solution)/shard_map/ppermute | solution.py:20
  54.8 2.2 gather_fusion.2
  57.0 34.6 %all-gather.5.cloned.1.call-done = bf16[8,128,896]{2,1,0:T(8,128)(2,1)} async-done(((bf16[1,128,896]{2,1,0:T(8,128)(2,1)}), bf16[8,128,896]{2,1,0:T(8,128)(2,1)}) %all-gather.5.cloned.1.call-update) | async-done | bytes 1835024 | tf_op jit(solution)/shard_map/all_gather | solution.py:24
  91.6 4.4 %collective-permute-start = (bf16[8,128,896]{2,1,0:T(8,128)(2,1)}, bf16[8,128,896]{2,1,0:T(8,128)(2,1)}, u32[]{:S(2)}, u32[]{:S(2)}) collective-permute-start(bf16[8,128,896]{2,1,0:T(8,128)(2,1)} %all-gather.5.cloned.1.call-done), channel_id=1, source_target_pairs={{0,16},{16,0},{1,17},{17,1},{2,18},{18,2},{3,19},{19,3},{4,20},{20... | collective-permute-start | bytes 5505032 | tf_op jit(solution)/shard_map/ppermute | solution.py:20
  96.0 36.5 %all-gather.7.cloned.1.call-done = bf16[8,128,896]{2,1,0:T(8,128)(2,1)} async-done(((bf16[1,128,896]{2,1,0:T(8,128)(2,1)}), bf16[8,128,896]{2,1,0:T(8,128)(2,1)}) %all-gather.7.cloned.1.call-update) | async-done | bytes 1835024 | tf_op jit(solution)/shard_map/all_gather | solution.py:24
  132.6 4.4 %collective-permute-start.1 = (bf16[8,128,896]{2,1,0:T(8,128)(2,1)}, bf16[8,128,896]{2,1,0:T(8,128)(2,1)}, u32[]{:S(2)}, u32[]{:S(2)}) collective-permute-start(bf16[8,128,896]{2,1,0:T(8,128)(2,1)} %all-gather.7.cloned.1.call-done), channel_id=1, source_target_pairs={{0,16},{16,0},{1,17},{17,1},{2,18},{18,2},{3,19},{19,3},{4,20},{20... | collective-permute-start | bytes 5505032 | tf_op jit(solution)/shard_map/ppermute | solution.py:20
  136.9 1.5 copy-done.2
  138.4 6.5 %all-to-all-start.3 = ((bf16[16,40,2048]{2,1,0:T(8,128)(2,1)}), bf16[16,40,2048]{2,1,0:T(8,128)(2,1)S(1)}, u32[]{:S(2)}, u32[]{:S(2)}) async-start(bf16[16,40,2048]{2,1,0:T(8,128)(2,1)} %gather_fusion.2), calls=%async_computation.3 | async-start | bytes 5242880 | tf_op jit(solution)/shard_map/all_to_all | solution.py:127
  145.0 4.8 %fusion.9 = f32[640,896]{1,0:T(8,128)} fusion(bf16[1024,896]{1,0:T(8,128)(2,1)} %bitcast.90, bf16[640,2048]{1,0:T(8,128)(2,1)} %bitcast.80), kind=kOutput, calls=%fused_computation.33 | convolution fusion | flops 1174405120 | bytes 5439488 | tf_op jit(solution)/shard_map/dot_general | solution.py:98
  149.8 23.7 %all-gather.9.cloned.1.call-done = bf16[8,56,2048]{2,1,0:T(8,128)(2,1)} async-done(((bf16[1,56,2048]{2,1,0:T(8,128)(2,1)}), bf16[8,56,2048]{2,1,0:T(8,128)(2,1)}) %all-gather.9.cloned.1.call-update) | async-done | bytes 1835024 | tf_op jit(solution)/shard_map/all_gather | solution.py:24
  173.5 3.8 %collective-permute-start.2 = (bf16[8,56,2048]{2,1,0:T(8,128)(2,1)}, bf16[8,56,2048]{2,1,0:T(8,128)(2,1)}, u32[]{:S(2)}, u32[]{:S(2)}) collective-permute-start(bf16[8,56,2048]{2,1,0:T(8,128)(2,1)} %all-gather.9.cloned.1.call-done), channel_id=1, source_target_pairs={{0,16},{16,0},{1,17},{17,1},{2,18},{18,2},{3,19},{19,3},{4,20},{20... | collective-permute-start | bytes 5505032 | tf_op jit(solution)/shard_map/ppermute | solution.py:20
  177.3 3.5 %fusion.7 = f32[640,896]{1,0:T(8,128)S(1)} fusion(bf16[1024,896]{1,0:T(8,128)(2,1)} %bitcast.91, bf16[640,2048]{1,0:T(8,128)(2,1)} %bitcast.81), kind=kOutput, calls=%fused_computation.31 | convolution fusion | flops 1174405120 | bytes 5439488 | tf_op jit(solution)/shard_map/dot_general | solution.py:98
  180.9 1.7 select_bitcast_fusion.2
  182.6 1.0 convert_multiply_fusion
  183.7 3.9 %copy.88 = f32[8,2,56,2048]{3,2,1,0:T(8,128)} copy(f32[8,2,56,2048]{3,2,0,1:T(8,128)S(1)} %convert_multiply_fusion) | data formatting | bytes 14680064 | tf_op jit(solution)/shard_map/mul | solution.py:135
  187.5 3.2 %fusion.5 = f32[640,896]{1,0:T(8,128)S(1)} fusion(bf16[1024,896]{1,0:T(8,128)(2,1)} %bitcast.9, bf16[640,2048]{1,0:T(8,128)(2,1)S(1)} %bitcast.82), kind=kOutput, calls=%fused_computation.29 | convolution fusion | flops 1174405120 | bytes 5439488 | tf_op jit(solution)/shard_map/dot_general | solution.py:100
  190.7 4.2 %multiply_convert_fusion.2 = bf16[640,896]{1,0:T(8,128)(2,1)} fusion(f32[640,896]{1,0:T(8,128)S(1)} %fusion.7, f32[640,896]{1,0:T(8,128)S(1)} %copy-done.9, f32[640,896]{1,0:T(8,128)S(1)} %fusion.5, bf16[1024,896]{1,0:T(8,128)(2,1)} %bitcast.11, bf16[640,2048]{1,0:T(8,128)(2,1)S(1)} %bitcast.83), kind=kOutput, calls=%fused_computation.20 | convolution fusion | flops 1178992640 | bytes 11173888 | tf_op jit(solution)/shard_map/dot_general | solution.py:100
  194.9 7.5 %abs_reduce_fusion = (f32[896]{0:T(1024)S(1)}, f32[896,2048]{1,0:T(8,128)S(1)}) fusion(bf16[1,1,896,2048]{3,2,1,0:T(8,128)(2,1)} %param.24, bf16[640,2048]{1,0:T(8,128)(2,1)S(1)} %bitcast.78, bf16[640,896]{1,0:T(8,128)(2,1)} %multiply_convert_fusion.2, f32[640]{0:T(1024)S(1)} %reshape.210, f32[8,2,56,2048]{3,2,1,0:T(8,128)} %copy.88), kind=kOutput, calls=%fused_computation.7 | convolution fusion | flops 2361539584 | bytes 22124544 | tf_op jit(solution)/shard_map/rh,rd->hd/dot_general | solution.py:133
  202.5 2.9 %fusion = (bf16[1,1,896,2048]{3,2,1,0:T(8,128)(2,1)}, bf16[896,2048]{1,0:T(8,128)(2,1)S(1)}) fusion(f32[896,2048]{1,0:T(8,128)S(1)} %get-tuple-element.18, f32[896]{0:T(1024)S(1)} %multiply_add_fusion.1), kind=kLoop, calls=%fused_computation.9 | loop fusion | flops 11010048 | bytes 14683648 | tf_op jit(solution)/shard_map/broadcast_in_dim | solution.py:138
  205.7 1.2 copy-done.7
  206.9 3.0 %select_bitcast_fusion.4 = (bf16[8,1,56,2048]{3,2,1,0:T(8,128)(2,1)S(1)}, bf16[8,1,56,2048]{3,2,1,0:T(8,128)(2,1)}) fusion(bf16[8,56,2048]{2,1,0:T(8,128)(2,1)S(1)} %copy-done.7, bf16[8,56,2048]{2,1,0:T(8,128)(2,1)} %collective-permute-done.2, pred[]{:T(512)S(6)} %eq.58), kind=kLoop, calls=%fused_computation.27 | loop fusion | flops 1835008 | bytes 7340033 | tf_op jit(solution)/shard_map/stack | solution.py:30
  209.9 2.4 fusion.1
  212.4 1.9 pad_maximum_fusion
  214.3 3.1 %convolution_convert_fusion = bf16[640,2048]{1,0:T(8,128)(2,1)S(1)} fusion(bf16[640,896]{1,0:T(8,128)(2,1)S(1)} %copy-done.4, bf16[896,2048]{1,0:T(8,128)(2,1)S(1)} %bitcast.79), kind=kOutput, calls=%fused_computation.13 | convolution fusion | flops 2350120960 | bytes 7438336 | tf_op jit(solution)/shard_map/dot_general | solution.py:109
  217.4 40.1 %all_to_all.21 = bf16[16,40,2048]{2,1,0:T(8,128)(2,1)S(1)} all-to-all(bf16[16,40,2048]{2,1,0:T(8,128)(2,1)S(1)} %bitcast.84), channel_id=1, replica_groups=mesh['z'=8,'core'=2,'expert'=16] {'expert'}, dimensions={0} | all-to-all | bytes 5242880 | tf_op jit(solution)/shard_map/all_to_all | solution.py:112
  257.5 3.0 %fusion.2 = f32[2,40,2048]{2,0,1:T(2,128)S(1)} fusion(bf16[16,2,1]{0,1,2:T(2,128)(2,1)S(1)} %copy-done.8, bf16[16,40,2048]{2,1,0:T(8,128)(2,1)S(1)} %all_to_all.21), kind=kOutput, calls=%fused_computation.14 | convolution fusion | flops 5242880 | bytes 3276864 | tf_op jit(solution)/shard_map/kcd,ke->ecd/dot_general | solution.py:119
  260.4 0.4 copy.87
  260.8 1.8 convolution_convert_fusion.1
  262.6 1.1 abs_reduce_fusion.1
  263.8 1.9 convert_subtract_fusion
  (52 shorter events, 2.0 us)
Async XLA Ops:
  7.2 47.3 %copy-start = (bf16[128,2048]{1,0:T(8,128)(2,1)S(1)}, bf16[128,2048]{1,0:T(8,128)(2,1)}, u32[]{:S(2)}) copy-start(bf16[128,2048]{1,0:T(8,128)(2,1)} %param.22) | copy-start | bytes 1572868
  7.2 43.4 %all-gather.11.cloned.1.call-start = ((), (), s32[]{:S(2)}) async-start(), calls=%async_computation.8 | async-start | bytes 2064384 | tf_op jit(solution)/shard_map/all_gather | solution.py:24
  7.9 83.7 %all-gather.5.cloned.1.call-start = ((), (), s32[]{:S(2)}) async-start(), calls=%async_computation.5 | async-start | bytes 2064384 | tf_op jit(solution)/shard_map/all_gather | solution.py:24
  8.7 123.9 %all-gather.7.cloned.1.call-start = ((), (), s32[]{:S(2)}) async-start(), calls=%async_computation.6 | async-start | bytes 2064384 | tf_op jit(solution)/shard_map/all_gather | solution.py:24
  15.0 13.9 %all-to-all-start.2 = ((bf16[16,1,40]{2,1,0:T(2,128)(2,1)}), bf16[16,1,40]{2,1,0:T(2,128)(2,1)S(1)}, u32[]{:S(2)}, u32[]{:S(2)}) async-start(bf16[16,1,40]{2,1,0:T(2,128)(2,1)} %copy.89), calls=%async_computation.2 | async-start | bytes 16384 | tf_op jit(solution)/shard_map/all_to_all | solution.py:90
  22.6 150.9 %all-gather.9.cloned.1.call-start = ((), (), s32[]{:S(2)}) async-start(), calls=%async_computation.7 | async-start | bytes 2064384 | tf_op jit(solution)/shard_map/all_gather | solution.py:24
  29.0 108.0 %all-to-all-start = ((bf16[16,40,2048]{2,1,0:T(8,128)(2,1)}), bf16[16,40,2048]{2,1,0:T(8,128)(2,1)S(1)}, u32[]{:S(2)}, u32[]{:S(2)}) async-start(bf16[16,40,2048]{2,1,0:T(8,128)(2,1)} %gather_fusion.1), calls=%async_computation | async-start | bytes 5242880 | tf_op jit(solution)/shard_map/all_to_all | solution.py:89
  50.6 130.3 %collective-permute-start.3 = (bf16[8,56,2048]{2,1,0:T(8,128)(2,1)}, bf16[8,56,2048]{2,1,0:T(8,128)(2,1)}, u32[]{:S(2)}, u32[]{:S(2)}) collective-permute-start(bf16[8,56,2048]{2,1,0:T(8,128)(2,1)} %all-gather.11.cloned.1.call-done), channel_id=1, source_target_pairs={{0,16},{16,0},{1,17},{17,1},{2,18},{18,2},{3,19},{19,3},{4,20},{20... | collective-permute-start | bytes 5505032 | tf_op jit(solution)/shard_map/ppermute | solution.py:20
  91.6 96.0 %collective-permute-start = (bf16[8,128,896]{2,1,0:T(8,128)(2,1)}, bf16[8,128,896]{2,1,0:T(8,128)(2,1)}, u32[]{:S(2)}, u32[]{:S(2)}) collective-permute-start(bf16[8,128,896]{2,1,0:T(8,128)(2,1)} %all-gather.5.cloned.1.call-done), channel_id=1, source_target_pairs={{0,16},{16,0},{1,17},{17,1},{2,18},{18,2},{3,19},{19,3},{4,20},{20... | collective-permute-start | bytes 5505032 | tf_op jit(solution)/shard_map/ppermute | solution.py:20
  132.6 58.1 %collective-permute-start.1 = (bf16[8,128,896]{2,1,0:T(8,128)(2,1)}, bf16[8,128,896]{2,1,0:T(8,128)(2,1)}, u32[]{:S(2)}, u32[]{:S(2)}) collective-permute-start(bf16[8,128,896]{2,1,0:T(8,128)(2,1)} %all-gather.7.cloned.1.call-done), channel_id=1, source_target_pairs={{0,16},{16,0},{1,17},{17,1},{2,18},{18,2},{3,19},{19,3},{4,20},{20... | collective-permute-start | bytes 5505032 | tf_op jit(solution)/shard_map/ppermute | solution.py:20
  136.9 1.5 copy-start.2
  138.4 56.5 %all-to-all-start.3 = ((bf16[16,40,2048]{2,1,0:T(8,128)(2,1)}), bf16[16,40,2048]{2,1,0:T(8,128)(2,1)S(1)}, u32[]{:S(2)}, u32[]{:S(2)}) async-start(bf16[16,40,2048]{2,1,0:T(8,128)(2,1)} %gather_fusion.2), calls=%async_computation.3 | async-start | bytes 5242880 | tf_op jit(solution)/shard_map/all_to_all | solution.py:127
  145.0 117.7 %reduce-scatter.2.cloned.1.call-start = ((), (), s32[]{:S(2)}) async-start(), calls=%async_computation.9 | async-start | bytes 2064384 | tf_op jit(solution)/shard_map/reduce_scatter | solution.py:145
  173.5 32.2 %collective-permute-start.2 = (bf16[8,56,2048]{2,1,0:T(8,128)(2,1)}, bf16[8,56,2048]{2,1,0:T(8,128)(2,1)}, u32[]{:S(2)}, u32[]{:S(2)}) collective-permute-start(bf16[8,56,2048]{2,1,0:T(8,128)(2,1)} %all-gather.9.cloned.1.call-done), channel_id=1, source_target_pairs={{0,16},{16,0},{1,17},{17,1},{2,18},{18,2},{3,19},{19,3},{4,20},{20... | collective-permute-start | bytes 5505032 | tf_op jit(solution)/shard_map/ppermute | solution.py:20
  177.3 3.6 %copy-start.6 = (bf16[8,56,2048]{2,1,0:T(8,128)(2,1)S(1)}, bf16[8,56,2048]{2,1,0:T(8,128)(2,1)}, u32[]{:S(2)}) copy-start(bf16[8,56,2048]{2,1,0:T(8,128)(2,1)} %all-gather.11.cloned.1.call-done) | copy-start | bytes 5505028
  183.6 3.9 %copy-start.3 = (bf16[16,40,2048]{2,1,0:T(8,128)(2,1)S(1)}, bf16[16,40,2048]{2,1,0:T(8,128)(2,1)}, u32[]{:S(2)}) copy-start(bf16[16,40,2048]{2,1,0:T(8,128)(2,1)} %copy-done.2) | copy-start | bytes 7864324
  187.5 3.2 %copy-start.9 = (f32[640,896]{1,0:T(8,128)S(1)}, f32[640,896]{1,0:T(8,128)}, u32[]{:S(2)}) copy-start(f32[640,896]{1,0:T(8,128)} %fusion.9) | copy-start | bytes 6881284
  205.4 1.5 copy-start.7
  205.6 4.3 %collective-permute-start.4 = (bf16[8,56,2048]{2,1,0:T(8,128)(2,1)S(1)}, bf16[8,56,2048]{2,1,0:T(8,128)(2,1)S(1)}, u32[]{:S(2)}, u32[]{:S(2)}) collective-permute-start(bf16[8,56,2048]{2,1,0:T(8,128)(2,1)S(1)} %select_bitcast_fusion), channel_id=1, source_target_pairs={{0,16},{16,0},{1,17},{17,1},{2,18},{18,2},{3,19},{19,3},{4,20},{20... | collective-permute-start | bytes 5505032 | tf_op jit(solution)/shard_map/ppermute | solution.py:20
  212.4 1.9 copy-start.4
  217.4 40.1 %copy-start.8 = (bf16[16,2,1]{0,1,2:T(2,128)(2,1)S(1)}, bf16[16,2,1]{0,1,2:T(2,128)(2,1)}, u32[]{:S(2)}) copy-start(bf16[16,2,1]{0,1,2:T(2,128)(2,1)} %constant.110) | copy-start | bytes 196
  257.5 5.2 %copy-start.5 = (f32[1,56,2048]{2,1,0:T(8,128)S(1)}, f32[1,56,2048]{2,1,0:T(8,128)}, u32[]{:S(2)}) copy-start(f32[1,56,2048]{2,1,0:T(8,128)} %param.25) | copy-start | bytes 1376260
  257.5 8.2 %copy-start.1 = (bf16[128,2048]{1,0:T(8,128)(2,1)S(1)}, bf16[128,2048]{1,0:T(8,128)(2,1)}, u32[]{:S(2)}) copy-start(bf16[128,2048]{1,0:T(8,128)(2,1)} %param.22) | copy-start | bytes 1572868
Sparse Core Ops, SparseCore 0:
  9.8 40.7 all-gather.10
  52.4 39.1 all-gather.4
  93.4 39.1 all-gather.6
  134.2 39.2 all-gather.8
  212.5 35.8 reduce-scatter.1
